TPU v7x, 256 devices: a whole 4x4x8 slice. The times are simulated.
256 devices in a mesh: section: 2 (over core), req: 16 (over x, y), head: 8 (over z).
Axes of the slice: x: 4, y: 4, z: 8, core: 2. Of those that a mesh axis runs over, the one named last changes fastest.
Arguments:
- tokens: bfloat16 [256, 8192], P(None, 'req'), may hold values from -14 to 14
- attention_gain: bfloat16 [2, 8192], P('section', 'req'), may hold values from 0.099609375 to 1.8984375
- query_key_value_weight: bfloat16 [2, 8192, 8, 1280], P('section', 'req', 'head'), may hold values from -0.0625 to 0.0625
- head_output_weight: bfloat16 [2, 8, 1024, 8192], P('section', 'head', None, 'req'), may hold values from -0.0625 to 0.0625
- feedforward_gain: bfloat16 [2, 8192], P('section', 'req'), may hold values from 0.099609375 to 1.8984375
- gate_up: bfloat16 [2, 8192, 2, 14336], P('section', 'req', None, 'head'), may hold values from -0.0625 to 0.0625
- down_weight: bfloat16 [2, 14336, 8192], P('section', 'head', 'req'), may hold values from -0.046875 to 0.046875
- packed_cache: bfloat16 [2, 32768, 8, 256], P('section', 'req', 'head'), may hold values from -70 to 70
- long_cache: bfloat16 [2, 2, 32768, 8, 256], P('section', None, 'req', 'head'), may hold values from -70 to 70
- lengths: int32 [16, 16], P('req'), may hold values from 1 to 256, 2048 in all within a row
- long_split: int32 [2, 16], P(None, 'req'), may hold values from 1 to 2048, 16384 in all within a row
Outputs:
- layer_outputs: bfloat16 [2, 256, 8192], P('section', None, 'req')
Inputs may be any that keep to these rules, and one draw needn't show every extreme that they name: Row g holds the lengths of the 16 requests of request group g in order; they sum to 2048, and the requests' keys fill that group's 2048 slots of packed_cache one request after another. `long_split`: entry (j, g) counts the live slots, the first ones, of group g's 2048 slots of long request j; each row sums to 16384.
All inputs are finite; a program needn't handle non-finite values.
Results may differ from a plain program's by a relative error of at most 0.04.
Values may be sent and summed in bfloat16 or wider, within the bound.
A program may use at most 64 MiB of HBM per device.

v0:
```python
import math
import jax
import jax.numpy as jnp
from jax import lax
from jax.sharding import PartitionSpec as P

MODEL_WIDTH = 8192
QUERY_HEADS = 64
KEY_VALUE_HEADS = 8
HEAD_SIZE = 128
LONG = 16384
EPSILON = 1e-05


def merged(part, axis, combine):
    gathered = jax.tree.map(lambda a: lax.all_gather(a, axis), part)

    def take(source):
        return jax.tree.map(lambda a: lax.dynamic_index_in_dim(a, source, 0, False), gathered)

    return lax.fori_loop(
        1, lax.axis_size(axis), lambda source, state: combine(state, take(source)), take(0)
    )


def shifted(value, axis, by):
    peers = lax.axis_size(axis)
    pairs = [(i, i + by) for i in range(peers) if 0 <= i + by < peers]
    return lax.ppermute(value, axis, pairs)


def rotate(values, position):
    half_dim = values.shape[-1] // 2
    freq_ids = jnp.arange(half_dim).astype(jnp.float32)
    inverse = 1.0 / 10000.0 ** (freq_ids * 2.0 / values.shape[-1])
    angles = position.astype(jnp.float32)[:, None] * inverse[None, :]
    cosine = jnp.cos(angles)[:, None, None, :]
    sine_part = jnp.sin(angles)[:, None, None, :]
    lower_half = values[..., :half_dim]
    upper_half = values[..., half_dim:]
    return jnp.concatenate(
        [
            lower_half * cosine - upper_half * sine_part,
            upper_half * cosine + lower_half * sine_part,
        ],
        -1,
    )


def add_pair(earlier, second_part):
    return earlier + second_part


def combine_partial(earlier, second_part):
    peak = jnp.maximum(earlier[0], second_part[0])
    left_factor = jnp.exp(earlier[0] - peak)
    right_factor = jnp.exp(second_part[0] - peak)
    softmax_total = earlier[1] * left_factor + second_part[1] * right_factor
    weighted_sum = earlier[2] * left_factor[..., None] + second_part[2] * right_factor[..., None]
    return (peak, softmax_total, weighted_sum)


def over_requests(values, combiner):
    return merged(values, "req", combiner)


def rows_apply(values, row_fn):
    return row_fn(lax.all_gather(values, "req", axis=0, tiled=True), jnp.int32(0))


def rows_project(term_fn, row_count):
    return lax.psum_scatter(
        term_fn(jnp.int32(0), row_count * lax.axis_size("req")),
        "req",
        scatter_dimension=0,
        tiled=True,
    )


def head_total(values):
    return lax.psum(values, "head")


def keep_rows(piece_rows, start_row):
    return piece_rows


def norm_rows(values, gain_row):
    floats = values.astype(jnp.float32)
    squares = over_requests(jnp.sum(floats * floats, axis=-1), add_pair)
    return (
        floats * lax.rsqrt(squares / MODEL_WIDTH + EPSILON)[:, None] * gain_row.astype(jnp.float32)
    ).astype(jnp.bfloat16)


def decoder_layer(
    inputs,
    micro_batch,
    attention_gain,
    query_key_value_weight,
    head_output_weight,
    feedforward_gain,
    gate_up,
    down_weight,
    packed_cache,
    long_cache,
    lengths,
    long_split,
):
    req_count = lax.axis_size("req")
    group_index = lax.axis_index("req")
    blocks = inputs.shape[0] // req_count
    columns = query_key_value_weight.shape[1]
    kv_local = query_key_value_weight.shape[2]
    requests_per_group = QUERY_HEADS // KEY_VALUE_HEADS
    score_scale = 1.0 / math.sqrt(HEAD_SIZE)
    normalized_input = norm_rows(inputs, attention_gain[0])
    in_weights = query_key_value_weight[0].reshape(
        columns, kv_local * (requests_per_group + 2) * HEAD_SIZE
    )

    def qkv_term(start_row, row_count):
        return jnp.dot(normalized_input, in_weights, preferred_element_type=jnp.float32)

    projected_rows = rows_project(qkv_term, blocks).reshape(
        blocks, kv_local, requests_per_group + 2, HEAD_SIZE
    )
    local_rows = jnp.arange(blocks)
    row_lengths = lengths[0]
    owner_long = (group_index == 0) | (group_index == req_count // 2)
    long_row = (local_rows == 0) & (micro_batch == 0) & owner_long
    position = row_lengths + jnp.where(long_row, LONG, 0).astype(jnp.int32)
    queries = rotate(projected_rows[:, :, :requests_per_group], position).astype(jnp.bfloat16)
    new_key = rotate(projected_rows[:, :, requests_per_group : requests_per_group + 1], position)[
        :, :, 0
    ].astype(jnp.bfloat16)
    new_value = projected_rows[:, :, requests_per_group + 1].astype(jnp.bfloat16)
    gathered = rows_apply(
        queries[0:1].reshape(1, kv_local * requests_per_group * HEAD_SIZE), keep_rows
    )
    long_queries = jnp.stack([gathered[0], gathered[req_count // 2]]).reshape(
        2, kv_local, requests_per_group, HEAD_SIZE
    )
    far_cache = long_cache[0]
    far_live = (jnp.arange(far_cache.shape[1])[None, :] < long_split[:, 0][:, None])[
        :, None, None, :
    ]
    far_scores = (
        jnp.einsum(
            "jkhd,jpkd->jkhp",
            long_queries,
            far_cache[..., :HEAD_SIZE],
            preferred_element_type=jnp.float32,
        )
        * score_scale
    )
    far_max = jnp.max(jnp.where(far_live, far_scores, -jnp.inf), axis=-1)
    far_weights = jnp.where(
        far_live, jnp.exp(jnp.where(far_live, far_scores - far_max[..., None], 0.0)), 0.0
    ).astype(jnp.bfloat16)
    far_totals = jnp.sum(far_weights.astype(jnp.float32), axis=-1)
    far_summed = jnp.einsum(
        "jkhp,jpkd->jkhd",
        far_weights,
        far_cache[..., HEAD_SIZE:],
        preferred_element_type=jnp.float32,
    )
    far_max, far_totals, far_summed = over_requests(
        (far_max, far_totals, far_summed), combine_partial
    )
    far_index = jnp.where(group_index == 0, 0, 1)
    chosen_max = lax.dynamic_index_in_dim(far_max, far_index, 0, keepdims=False)
    chosen_totals = lax.dynamic_index_in_dim(far_totals, far_index, 0, keepdims=False)
    chosen_summed = lax.dynamic_index_in_dim(far_summed, far_index, 0, keepdims=False)
    pack_part = packed_cache[0]
    seg_ends = jnp.cumsum(lengths[0])
    slot_ids = jnp.arange(pack_part.shape[0])
    slot_owner = jnp.sum((slot_ids[:, None] >= seg_ends[None, :]).astype(jnp.int32), axis=1)
    request_ids = micro_batch * blocks + local_rows
    in_segment = (slot_owner[None, :] == request_ids[:, None])[:, None, None, :]
    scores = (
        jnp.einsum(
            "rkhd,pkd->rkhp",
            queries,
            pack_part[..., :HEAD_SIZE],
            preferred_element_type=jnp.float32,
        )
        * score_scale
    )
    own_score = (
        jnp.einsum("rkhd,rkd->rkh", queries, new_key, preferred_element_type=jnp.float32)
        * score_scale
    )
    row_max = jnp.maximum(jnp.max(jnp.where(in_segment, scores, -jnp.inf), axis=-1), own_score)
    long_mask = long_row[:, None, None]
    row_max = jnp.where(long_mask, jnp.maximum(row_max, chosen_max[None]), row_max)
    weights = jnp.where(
        in_segment, jnp.exp(jnp.where(in_segment, scores - row_max[..., None], 0.0)), 0.0
    ).astype(jnp.bfloat16)
    own_weights = jnp.exp(own_score - row_max).astype(jnp.bfloat16)
    far_factor = jnp.where(
        long_mask, jnp.exp(jnp.where(long_mask, chosen_max[None] - row_max, 0.0)), 0.0
    )
    softmax_total = (
        jnp.sum(weights.astype(jnp.float32), axis=-1)
        + own_weights.astype(jnp.float32)
        + far_factor * chosen_totals[None]
    )
    weighted_sum = jnp.einsum(
        "rkhp,pkd->rkhd", weights, pack_part[..., HEAD_SIZE:], preferred_element_type=jnp.float32
    )
    weighted_sum = (
        weighted_sum
        + own_weights.astype(jnp.float32)[..., None] * new_value.astype(jnp.float32)[:, :, None, :]
    )
    weighted_sum = weighted_sum + far_factor[..., None] * chosen_summed[None]
    attended_heads = (
        (weighted_sum / softmax_total[..., None])
        .astype(jnp.bfloat16)
        .reshape(blocks, kv_local * requests_per_group * HEAD_SIZE)
    )
    out_weights = head_output_weight[0].reshape(kv_local * requests_per_group * HEAD_SIZE, columns)

    def project_heads(piece_rows, start_row):
        return jnp.dot(piece_rows, out_weights, preferred_element_type=jnp.float32)

    attended = head_total(rows_apply(attended_heads, project_heads))
    residual = (inputs.astype(jnp.float32) + attended).astype(jnp.bfloat16)
    normed_two = norm_rows(residual, feedforward_gain[0])
    ff_weights = gate_up[0].reshape(columns, -1)

    def ff_term(start_row, row_count):
        return jnp.dot(normed_two, ff_weights, preferred_element_type=jnp.float32)

    gate_and_up = rows_project(ff_term, blocks)
    hidden_width = gate_and_up.shape[1] // 2
    hidden = (jax.nn.silu(gate_and_up[:, :hidden_width]) * gate_and_up[:, hidden_width:]).astype(
        jnp.bfloat16
    )
    lower_weights = down_weight[0]

    def project_hidden(piece_rows, start_row):
        return jnp.dot(piece_rows, lower_weights, preferred_element_type=jnp.float32)

    lowered = head_total(rows_apply(hidden, project_hidden))
    return (residual.astype(jnp.float32) + lowered).astype(jnp.bfloat16)


def local(
    tokens,
    attention_gain,
    query_key_value_weight,
    head_output_weight,
    feedforward_gain,
    gate_up,
    down_weight,
    packed_cache,
    long_cache,
    lengths,
    long_split,
):
    req_count = lax.axis_size("req")
    section_index = lax.axis_index("section")
    batch_count = 1
    per_group = tokens.shape[0] // req_count
    blocks = per_group // batch_count
    columns = tokens.shape[1]
    token_grid = tokens.reshape(req_count, per_group, columns)
    result = jnp.zeros_like(token_grid)
    incoming = jnp.zeros((req_count * blocks, columns), jnp.bfloat16)
    for phase_step in range(batch_count + 1):
        micro_batch = phase_step - section_index
        is_active = (micro_batch >= 0) & (micro_batch < batch_count)
        micro_batch = jnp.clip(micro_batch, 0, batch_count - 1)
        new_batch = token_grid.reshape(req_count * blocks, columns)
        inputs = jnp.where(section_index == 0, new_batch, incoming)
        output = decoder_layer(
            inputs,
            micro_batch,
            attention_gain,
            query_key_value_weight,
            head_output_weight,
            feedforward_gain,
            gate_up,
            down_weight,
            packed_cache,
            long_cache,
            lengths,
            long_split,
        )
        placed = output.reshape(req_count, blocks, columns)
        result = jnp.where(is_active, placed, result)
        if phase_step < batch_count:
            incoming = shifted(output, "section", 1)
    return result.reshape(1, req_count * per_group, columns)


def solution(mesh):
    placed = (
        P(None, "req"),
        P("section", "req"),
        P("section", "req", "head", None),
        P("section", "head", None, "req"),
        P("section", "req"),
        P("section", "req", None, "head"),
        P("section", "head", "req"),
        P("section", "req", "head", None),
        P("section", None, "req", "head", None),
        P("req", None),
        P(None, "req"),
    )
    return jax.shard_map(
        local, mesh=mesh, in_specs=placed, out_specs=P("section", None, "req"), check_vma=False
    )
```

profile of v0, /device:TPU:2, one launch (start us, length us, event | category | flops | bytes accessed | tf_op | source)
XLA Modules:
  0.0 1032.9 jit_solution(9253363095233518662)
XLA Ops:
  6.5 1.2 fusion.34
  7.8 23.3 %all-gather.10 = f32[16,1,256]{2,1,0:T(1,128)S(1)} all-gather(f32[1,1,256]{2,1,0:T(1,128)S(1)} %bitcast.379), channel_id=2, replica_groups=mesh['section'=2,'req'=16,'head'=8] {'req'}, dimensions={0}, use_global_device_ids=true | all-gather | bytes 17408 | tf_op jit(solution)/shard_map/all_gather | solution.py:16
  32.5 3.0 fusion.18
  36.4 78.1 %reduce-scatter.5.cloned.1.call-done = f32[16,1280]{1,0:T(8,128)} async-done(((f32[256,1280]{1,0:T(8,128)}), f32[16,1280]{1,0:T(8,128)}) %reduce-scatter.5.cloned.1.call-update) | async-done | bytes 81936 | tf_op jit(solution)/shard_map/reduce_scatter | solution.py:72
  115.7 21.4 %all-gather.11 = bf16[16,1,1024]{2,1,0:T(2,128)(2,1)S(1)} all-gather(bf16[1,1,1024]{2,1,0:T(2,128)(2,1)S(1)} %reshape.774), channel_id=1, replica_groups=mesh['section'=2,'req'=16,'head'=8] {'req'}, dimensions={0}, use_global_device_ids=true | all-gather | bytes 34816 | tf_op jit(solution)/shard_map/all_gather | solution.py:68
  137.2 1.7 select_reduce_fusion.3
  139.1 1.5 fusion.33
  140.6 22.6 %all-gather.12 = f32[16,2,8]{2,1,0:T(2,128)S(1)} all-gather(f32[1,2,8]{2,1,0:T(2,128)S(1)} %bitcast.371), channel_id=3, replica_groups=mesh['section'=2,'req'=16,'head'=8] {'req'}, dimensions={0}, use_global_device_ids=true | all-gather | bytes 1088 | tf_op jit(solution)/shard_map/all_gather | solution.py:16
  163.2 21.1 %all-gather.13 = f32[16,2,8]{2,1,0:T(2,128)S(1)} all-gather(f32[1,2,8]{2,1,0:T(2,128)S(1)} %bitcast.375), channel_id=4, replica_groups=mesh['section'=2,'req'=16,'head'=8] {'req'}, dimensions={0}, use_global_device_ids=true | all-gather | bytes 1088 | tf_op jit(solution)/shard_map/all_gather | solution.py:16
  184.3 23.0 %all-gather.3 = f32[32,8,128]{2,1,0:T(8,128)S(1)} all-gather(f32[2,8,128]{2,1,0:T(8,128)S(1)} %fusion.33), channel_id=5, replica_groups=mesh['section'=2,'req'=16,'head'=8] {'req'}, dimensions={0}, use_global_device_ids=true | all-gather | bytes 139264 | tf_op jit(solution)/shard_map/all_gather | solution.py:16
  207.4 1.7 while.99
  211.0 21.7 %all_gather.87 = bf16[256,1024]{1,0:T(8,128)(2,1)S(1)} all-gather(bf16[16,1024]{1,0:T(8,128)(2,1)S(1)} %bitcast.340), channel_id=1, replica_groups=mesh['section'=2,'req'=16,'head'=8] {'req'}, dimensions={0}, use_global_device_ids=true | all-gather | bytes 557056 | tf_op jit(solution)/shard_map/all_gather | solution.py:68
  232.7 1.3 fusion.30
  234.1 4.5 copy.75
  238.6 69.5 %all-reduce.5.cloned.1.call-done = f32[256,512]{1,0:T(8,128)} async-done(((f32[256,512]{1,0:T(8,128)}), f32[256,512]{1,0:T(8,128)}) %all-reduce.5.cloned.1.call-update) | async-done | bytes 524304 | tf_op jit(solution)/shard_map/psum | solution.py:81
  308.0 1.2 fusion.38
  309.3 23.0 %all-gather.14 = f32[16,1,256]{2,1,0:T(1,128)S(1)} all-gather(f32[1,1,256]{2,1,0:T(1,128)S(1)} %bitcast.378), channel_id=6, replica_groups=mesh['section'=2,'req'=16,'head'=8] {'req'}, dimensions={0}, use_global_device_ids=true | all-gather | bytes 17408 | tf_op jit(solution)/shard_map/all_gather | solution.py:16
  333.0 5.0 fusion.57
  338.1 77.9 %reduce-scatter.7.cloned.1.call-done = f32[16,3584]{1,0:T(8,128)} async-done(((f32[256,3584]{1,0:T(8,128)}), f32[16,3584]{1,0:T(8,128)}) %reduce-scatter.7.cloned.1.call-update) | async-done | bytes 229392 | tf_op jit(solution)/shard_map/reduce_scatter | solution.py:72
  416.0 1.0 fusion.70
  417.0 23.0 %all_gather.90 = bf16[256,1792]{1,0:T(8,128)(2,1)S(1)} all-gather(bf16[16,1792]{1,0:T(8,128)(2,1)S(1)} %fusion.70), channel_id=1, replica_groups=mesh['section'=2,'req'=16,'head'=8] {'req'}, dimensions={0}, use_global_device_ids=true | all-gather | bytes 974848 | tf_op jit(solution)/shard_map/all_gather | solution.py:68
  440.1 1.4 fusion.14
  441.6 73.4 %all-reduce.7.cloned.1.call-done = f32[256,512]{1,0:T(8,128)} async-done(((f32[256,512]{1,0:T(8,128)}), f32[256,512]{1,0:T(8,128)}) %all-reduce.7.cloned.1.call-update) | async-done | bytes 524304 | tf_op jit(solution)/shard_map/psum | solution.py:81
  515.0 1.9 fusion.41
  516.9 2.0 collective-permute-start
  520.5 23.0 %all-gather.15 = f32[16,1,256]{2,1,0:T(1,128)S(1)} all-gather(f32[1,1,256]{2,1,0:T(1,128)S(1)} %bitcast.376), channel_id=7, replica_groups=mesh['section'=2,'req'=16,'head'=8] {'req'}, dimensions={0}, use_global_device_ids=true | all-gather | bytes 17408 | tf_op jit(solution)/shard_map/all_gather | solution.py:16
  544.2 2.6 fusion.16
  546.8 74.6 %reduce-scatter.9.cloned.1.call-done = f32[16,1280]{1,0:T(8,128)} async-done(((f32[256,1280]{1,0:T(8,128)}), f32[16,1280]{1,0:T(8,128)}) %reduce-scatter.9.cloned.1.call-update) | async-done | bytes 81936 | tf_op jit(solution)/shard_map/reduce_scatter | solution.py:72
  622.6 21.5 %all-gather.16 = bf16[16,1,1024]{2,1,0:T(2,128)(2,1)S(1)} all-gather(bf16[1,1,1024]{2,1,0:T(2,128)(2,1)S(1)} %reshape.784), channel_id=1, replica_groups=mesh['section'=2,'req'=16,'head'=8] {'req'}, dimensions={0}, use_global_device_ids=true | all-gather | bytes 34816 | tf_op jit(solution)/shard_map/all_gather | solution.py:68
  644.1 1.7 select_reduce_fusion.2
  646.0 1.5 fusion.32
  647.7 1.5 select_reduce_fusion
  649.5 22.6 %all-gather.17 = f32[16,2,8]{2,1,0:T(2,128)S(1)} all-gather(f32[1,2,8]{2,1,0:T(2,128)S(1)} %bitcast.370), channel_id=8, replica_groups=mesh['section'=2,'req'=16,'head'=8] {'req'}, dimensions={0}, use_global_device_ids=true | all-gather | bytes 1088 | tf_op jit(solution)/shard_map/all_gather | solution.py:16
  672.1 21.1 %all-gather.18 = f32[16,2,8]{2,1,0:T(2,128)S(1)} all-gather(f32[1,2,8]{2,1,0:T(2,128)S(1)} %bitcast.374), channel_id=9, replica_groups=mesh['section'=2,'req'=16,'head'=8] {'req'}, dimensions={0}, use_global_device_ids=true | all-gather | bytes 1088 | tf_op jit(solution)/shard_map/all_gather | solution.py:16
  693.2 22.9 %all-gather.8 = f32[32,8,128]{2,1,0:T(8,128)S(1)} all-gather(f32[2,8,128]{2,1,0:T(8,128)S(1)} %fusion.32), channel_id=10, replica_groups=mesh['section'=2,'req'=16,'head'=8] {'req'}, dimensions={0}, use_global_device_ids=true | all-gather | bytes 139264 | tf_op jit(solution)/shard_map/all_gather | solution.py:16
  716.1 1.7 while.102
  718.4 1.5 fusion.26
  719.9 22.1 %all_gather.100 = bf16[256,1024]{1,0:T(8,128)(2,1)S(1)} all-gather(bf16[16,1024]{1,0:T(8,128)(2,1)S(1)} %bitcast.341), channel_id=1, replica_groups=mesh['section'=2,'req'=16,'head'=8] {'req'}, dimensions={0}, use_global_device_ids=true | all-gather | bytes 557056 | tf_op jit(solution)/shard_map/all_gather | solution.py:68
  742.0 1.2 fusion.28
  743.4 73.8 %all-reduce.9.cloned.1.call-done = f32[256,512]{1,0:T(8,128)} async-done(((f32[256,512]{1,0:T(8,128)}), f32[256,512]{1,0:T(8,128)}) %all-reduce.9.cloned.1.call-update) | async-done | bytes 524304 | tf_op jit(solution)/shard_map/psum | solution.py:81
  817.2 1.2 fusion.46
  818.4 23.0 %all-gather.19 = f32[16,1,256]{2,1,0:T(1,128)S(1)} all-gather(f32[1,1,256]{2,1,0:T(1,128)S(1)} %bitcast.377), channel_id=11, replica_groups=mesh['section'=2,'req'=16,'head'=8] {'req'}, dimensions={0}, use_global_device_ids=true | all-gather | bytes 17408 | tf_op jit(solution)/shard_map/all_gather | solution.py:16
  842.1 5.0 fusion.54
  847.2 78.0 %reduce-scatter.11.cloned.1.call-done = f32[16,3584]{1,0:T(8,128)} async-done(((f32[256,3584]{1,0:T(8,128)}), f32[16,3584]{1,0:T(8,128)}) %reduce-scatter.11.cloned.1.call-update) | async-done | bytes 229392 | tf_op jit(solution)/shard_map/reduce_scatter | solution.py:72
  926.2 23.0 %all_gather.103 = bf16[256,1792]{1,0:T(8,128)(2,1)S(1)} all-gather(bf16[16,1792]{1,0:T(8,128)(2,1)S(1)} %fusion.69), channel_id=1, replica_groups=mesh['section'=2,'req'=16,'head'=8] {'req'}, dimensions={0}, use_global_device_ids=true | all-gather | bytes 974848 | tf_op jit(solution)/shard_map/all_gather | solution.py:68
  949.2 1.5 fusion.12
  950.7 73.4 %all-reduce.11.cloned.1.call-done = f32[256,512]{1,0:T(8,128)} async-done(((f32[256,512]{1,0:T(8,128)}), f32[256,512]{1,0:T(8,128)}) %all-reduce.11.cloned.1.call-update) | async-done | bytes 524304 | tf_op jit(solution)/shard_map/psum | solution.py:81
  1024.1 1.9 fusion.53
  (354 shorter events, 17.5 us)
Async XLA Ops:
  6.5 433.5 %copy-start = (bf16[1,1792,512]{2,1,0:T(8,128)(2,1)S(1)}, bf16[1,1792,512]{2,1,0:T(8,128)(2,1)}, u32[]{:S(2)}) copy-start(bf16[1,1792,512]{2,1,0:T(8,128)(2,1)} %param.29) | copy-start | bytes 5505028
  6.5 108.0 %reduce-scatter.5.cloned.1.call-start = ((), (), s32[]{:S(2)}) async-start(), calls=%async_computation.4 | async-start | bytes 1392640 | tf_op jit(solution)/shard_map/reduce_scatter | solution.py:72
  32.5 3.2 copy-start.9
  32.5 3.7 copy-start.10
  35.6 272.5 %all-reduce.5.cloned.1.call-start = ((), (), s32[]{:S(2)}) async-start(), calls=%async_computation.5 | async-start | bytes 1048576 | tf_op jit(solution)/shard_map/psum | solution.py:81
  35.9 173.5 %copy-start.7 = (bf16[1,2048,1,256]{3,1,2,0:T(8,128)(2,1)S(1)}, bf16[1,2048,1,256]{3,1,2,0:T(8,128)(2,1)}, u32[]{:S(2)}) copy-start(bf16[1,2048,1,256]{3,1,2,0:T(8,128)(2,1)} %param.30) | copy-start | bytes 3145732
  210.1 22.7 %copy-start.3 = (bf16[1,1,1024,512]{3,2,1,0:T(8,128)(2,1)S(1)}, bf16[1,1,1024,512]{3,2,1,0:T(8,128)(2,1)}, u32[]{:S(2)}) copy-start(bf16[1,1,1024,512]{3,2,1,0:T(8,128)(2,1)} %param.26) | copy-start | bytes 3145732
  234.0 182.0 %reduce-scatter.7.cloned.1.call-start = ((), (), s32[]{:S(2)}) async-start(), calls=%async_computation.6 | async-start | bytes 3899392 | tf_op jit(solution)/shard_map/reduce_scatter | solution.py:72
  234.1 4.5 copy-start.8
  234.1 74.0 %copy-start.2 = (bf16[256,512]{1,0:T(8,128)(2,1)S(1)}, bf16[256,512]{1,0:T(8,128)(2,1)}, u32[]{:S(2)}) copy-start(bf16[256,512]{1,0:T(8,128)(2,1)} %param.23) | copy-start | bytes 786436
  309.3 28.8 %copy-start.5 = (bf16[256,512]{1,0:T(8,128)(2,1)}, bf16[256,512]{1,0:T(8,128)(2,1)S(1)}, u32[]{:S(2)}) copy-start(bf16[256,512]{1,0:T(8,128)(2,1)S(1)} %get-tuple-element.859) | copy-start | bytes 786436
  338.1 176.9 %all-reduce.7.cloned.1.call-start = ((), (), s32[]{:S(2)}) async-start(), calls=%async_computation.7 | async-start | bytes 1048576 | tf_op jit(solution)/shard_map/psum | solution.py:81
  441.5 102.7 %copy-start.1 = (bf16[1,512,1,1280]{3,1,2,0:T(8,128)(2,1)S(1)}, bf16[1,512,1,1280]{3,1,2,0:T(8,128)(2,1)}, u32[]{:S(2)}) copy-start(bf16[1,512,1,1280]{3,1,2,0:T(8,128)(2,1)} %param.25) | copy-start | bytes 3932164
  441.5 179.9 %reduce-scatter.9.cloned.1.call-start = ((), (), s32[]{:S(2)}) async-start(), calls=%async_computation.8 | async-start | bytes 1392640 | tf_op jit(solution)/shard_map/reduce_scatter | solution.py:72
  516.9 2.8 collective-permute-start
  546.8 270.4 %all-reduce.9.cloned.1.call-start = ((), (), s32[]{:S(2)}) async-start(), calls=%async_computation.9 | async-start | bytes 1048576 | tf_op jit(solution)/shard_map/psum | solution.py:81
  717.9 24.1 %copy-start.4 = (bf16[1,1,1024,512]{3,2,1,0:T(8,128)(2,1)S(1)}, bf16[1,1,1024,512]{3,2,1,0:T(8,128)(2,1)}, u32[]{:S(2)}) copy-start(bf16[1,1,1024,512]{3,2,1,0:T(8,128)(2,1)} %param.26) | copy-start | bytes 3145732
  719.9 97.2 %copy-start.6 = (bf16[256,512]{1,0:T(8,128)(2,1)S(1)}, bf16[256,512]{1,0:T(8,128)(2,1)}, u32[]{:S(2)}) copy-start(bf16[256,512]{1,0:T(8,128)(2,1)} %get-tuple-element.857) | copy-start | bytes 786436
  743.3 181.8 %reduce-scatter.11.cloned.1.call-start = ((), (), s32[]{:S(2)}) async-start(), calls=%async_computation.10 | async-start | bytes 3899392 | tf_op jit(solution)/shard_map/reduce_scatter | solution.py:72
  847.2 176.9 %all-reduce.11.cloned.1.call-start = ((), (), s32[]{:S(2)}) async-start(), calls=%async_computation.11 | async-start | bytes 1048576 | tf_op jit(solution)/shard_map/psum | solution.py:81
Sparse Core Ops, SparseCore 0:
  35.7 78.7 reduce-scatter.4
  234.1 73.8 all-reduce.4
  338.2 77.7 reduce-scatter.6
  441.6 73.2 all-reduce.6
  546.9 74.4 reduce-scatter.8
  743.4 73.6 all-reduce.8
  847.3 77.8 reduce-scatter.10
  950.8 73.2 all-reduce.10
where the time goes:
time: 1030 us
  waiting for transfers between devices  600 us (58%)
  blocking collectives  358 us (35%)
  matrix products  31.8 us (3%)
  other arithmetic  17.6 us (2%)
  between operations  13.9 us (1%)
    reduce_scatter x4, waiting for transfers between devices, rows_project(): lax.psum_scatter(term_fn(jnp.int32(0), row_count * lax.axis_size('req')),...  309 us
    psum x4, waiting for transfers between devices, head_total(): return lax.psum(values, 'head')  290 us
    all_gather x10, blocking collectives, merged(): gathered = jax.tree.map(lambda a: lax.all_gather(a, axis), part)  226 us
    all_gather x6, blocking collectives, rows_apply(): lax.all_gather(values, 'req', axis=0, tiled=True)  133 us
  transfers between devices with their start and end apart: 9, of which 9 were waited for; matrix products, arithmetic and copies ran while one was open for 1% of the time, Pallas kernels for 0%

commit v1 on v0

--- a/solution.py
+++ b/solution.py
@@ -10,6 +10,18 @@
 HEAD_SIZE = 128
 LONG = 16384
 EPSILON = 1e-05
+
+
+def _start_members_all(q_in):
+    link_axis = "req"
+    many = lax.axis_size(link_axis)
+    all_rows = []
+    for u in range(q_in.ndim):
+        all_rows.append(many if u == 0 else 1)
+    carry = lax.all_to_all(
+        jnp.tile(q_in, all_rows), link_axis, concat_axis=0, split_axis=0, tiled=True
+    )
+    return carry
 
 
 def merged(part, axis, combine):
@@ -65,7 +77,7 @@
 
 
 def rows_apply(values, row_fn):
-    return row_fn(lax.all_gather(values, "req", axis=0, tiled=True), jnp.int32(0))
+    return row_fn(_start_members_all(values), jnp.int32(0))
 
 
 def rows_project(term_fn, row_count):

time: 1030 us -> 987 us (0.958)
  blocking collectives: 358 us -> 288 us
  starting transfers between devices: 2.28 us -> 13.7 us
    all_gather x6 -> x0, blocking collectives: 133 us -> none  [rows_apply(): lax.all_gather(values, 'req', axis=0, tiled=True)]
    all_to_all x0 -> x4, blocking collectives: none -> 61.2 us  [_start_members_all(): lax.all_to_all(jnp.tile(q_in, all_rows), link_axis, concat_axis=0, split_...]
    all_to_all x0 -> x2, starting transfers between devices: none -> 11.4 us  [_start_members_all(): lax.all_to_all(jnp.tile(q_in, all_rows), link_axis, concat_axis=0, split_...]
  transfers between devices with their start and end apart: 9 -> 11, of which waited for: 9 -> 11; matrix products, arithmetic and copies ran while one was open for 1% -> 1% of each run, Pallas kernels for 0% -> 0%
where the time goes in v1:
time: 987 us; the launch traced here: 986 us
  waiting for transfers between devices  606 us (61%)
  blocking collectives  288 us (29%)
  matrix products  34.1 us (3%)
  other arithmetic  19.3 us (2%)
  between operations  13.9 us (1%)
  starting transfers between devices  13.7 us (1%)
    reduce_scatter x4, waiting for transfers between devices, rows_project(): lax.psum_scatter(term_fn(jnp.int32(0), row_count * lax.axis_size('req')),...  308 us
    psum x4, waiting for transfers between devices, head_total(): return lax.psum(values, 'head')  288 us
    all_gather x10, blocking collectives, merged(): gathered = jax.tree.map(lambda a: lax.all_gather(a, axis), part)  226 us
    all_to_all x4, blocking collectives, _start_members_all(): lax.all_to_all(jnp.tile(q_in, all_rows), link_axis, concat_axis=0, split_...  61.2 us
  transfers between devices with their start and end apart: 11, of which 11 were waited for; matrix products, arithmetic and copies ran while one was open for 1% of the time, Pallas kernels for 0%

profile of v1, /device:TPU:2, one launch (start us, length us, event | category | flops | bytes accessed | tf_op | source)
XLA Modules:
  0.0 986.1 jit_solution(3263592667374714678)
XLA Ops:
  7.8 23.3 %all-gather.10 = f32[16,1,256]{2,1,0:T(1,128)S(1)} all-gather(f32[1,1,256]{2,1,0:T(1,128)S(1)} %bitcast.369), channel_id=2, replica_groups=mesh['section'=2,'req'=16,'head'=8] {'req'}, dimensions={0}, use_global_device_ids=true | all-gather | bytes 17408 | tf_op jit(solution)/shard_map/all_gather | solution.py:28
  32.5 3.0 fusion.18
  36.4 78.2 %reduce-scatter.5.cloned.1.call-done = f32[16,1280]{1,0:T(8,128)} async-done(((f32[256,1280]{1,0:T(8,128)}), f32[16,1280]{1,0:T(8,128)}) %reduce-scatter.5.cloned.1.call-update) | async-done | bytes 81936 | tf_op jit(solution)/shard_map/reduce_scatter | solution.py:84
  117.9 5.7 all-to-all-start
  124.0 1.5 select_reduce_fusion.1
  125.5 4.3 all-to-all-done
  129.9 1.7 select_reduce_fusion.3
  131.8 1.5 fusion.33
  133.3 21.7 %all-gather.11 = f32[16,2,8]{2,1,0:T(2,128)S(1)} all-gather(f32[1,2,8]{2,1,0:T(2,128)S(1)} %bitcast.357), channel_id=3, replica_groups=mesh['section'=2,'req'=16,'head'=8] {'req'}, dimensions={0}, use_global_device_ids=true | all-gather | bytes 1088 | tf_op jit(solution)/shard_map/all_gather | solution.py:28
  155.0 21.4 %all-gather.12 = f32[16,2,8]{2,1,0:T(2,128)S(1)} all-gather(f32[1,2,8]{2,1,0:T(2,128)S(1)} %bitcast.365), channel_id=4, replica_groups=mesh['section'=2,'req'=16,'head'=8] {'req'}, dimensions={0}, use_global_device_ids=true | all-gather | bytes 1088 | tf_op jit(solution)/shard_map/all_gather | solution.py:28
  176.4 23.8 %all-gather.3 = f32[32,8,128]{2,1,0:T(8,128)S(1)} all-gather(f32[2,8,128]{2,1,0:T(8,128)S(1)} %fusion.33), channel_id=5, replica_groups=mesh['section'=2,'req'=16,'head'=8] {'req'}, dimensions={0}, use_global_device_ids=true | all-gather | bytes 139264 | tf_op jit(solution)/shard_map/all_gather | solution.py:28
  200.3 1.7 while.99
  202.6 1.6 fusion.27
  204.2 13.1 %all_to_all.48 = bf16[16,16,1024]{2,1,0:T(8,128)(2,1)S(1)} all-to-all(bf16[16,16,1024]{2,1,0:T(8,128)(2,1)S(1)} %tile.23), channel_id=1, replica_groups=mesh['section'=2,'req'=16,'head'=8] {'req'}, dimensions={0} | all-to-all | bytes 1048576 | tf_op jit(solution)/shard_map/all_to_all | solution.py:21
  217.3 1.2 fusion.30
  218.7 4.5 copy.74
  223.2 68.7 %all-reduce.5.cloned.1.call-done = f32[256,512]{1,0:T(8,128)} async-done(((f32[256,512]{1,0:T(8,128)}), f32[256,512]{1,0:T(8,128)}) %all-reduce.5.cloned.1.call-update) | async-done | bytes 524304 | tf_op jit(solution)/shard_map/psum | solution.py:93
  293.1 23.0 %all-gather.13 = f32[16,1,256]{2,1,0:T(1,128)S(1)} all-gather(f32[1,1,256]{2,1,0:T(1,128)S(1)} %bitcast.368), channel_id=6, replica_groups=mesh['section'=2,'req'=16,'head'=8] {'req'}, dimensions={0}, use_global_device_ids=true | all-gather | bytes 17408 | tf_op jit(solution)/shard_map/all_gather | solution.py:28
  316.8 5.0 fusion.57
  321.9 77.9 %reduce-scatter.7.cloned.1.call-done = f32[16,3584]{1,0:T(8,128)} async-done(((f32[256,3584]{1,0:T(8,128)}), f32[16,3584]{1,0:T(8,128)}) %reduce-scatter.7.cloned.1.call-update) | async-done | bytes 229392 | tf_op jit(solution)/shard_map/reduce_scatter | solution.py:84
  400.9 17.5 %all_to_all.49 = bf16[16,16,1792]{2,1,0:T(8,128)(2,1)S(1)} all-to-all(bf16[16,16,1792]{2,1,0:T(8,128)(2,1)S(1)} %tile.24), channel_id=1, replica_groups=mesh['section'=2,'req'=16,'head'=8] {'req'}, dimensions={0} | all-to-all | bytes 1835008 | tf_op jit(solution)/shard_map/all_to_all | solution.py:21
  418.4 1.4 fusion.14
  419.9 73.1 %all-reduce.7.cloned.1.call-done = f32[256,512]{1,0:T(8,128)} async-done(((f32[256,512]{1,0:T(8,128)}), f32[256,512]{1,0:T(8,128)}) %all-reduce.7.cloned.1.call-update) | async-done | bytes 524304 | tf_op jit(solution)/shard_map/psum | solution.py:93
  493.0 1.9 fusion.41
  494.9 2.0 collective-permute-start
  498.5 23.0 %all-gather.14 = f32[16,1,256]{2,1,0:T(1,128)S(1)} all-gather(f32[1,1,256]{2,1,0:T(1,128)S(1)} %bitcast.366), channel_id=7, replica_groups=mesh['section'=2,'req'=16,'head'=8] {'req'}, dimensions={0}, use_global_device_ids=true | all-gather | bytes 17408 | tf_op jit(solution)/shard_map/all_gather | solution.py:28
  522.2 2.6 fusion.16
  524.8 74.7 %reduce-scatter.9.cloned.1.call-done = f32[16,1280]{1,0:T(8,128)} async-done(((f32[256,1280]{1,0:T(8,128)}), f32[16,1280]{1,0:T(8,128)}) %reduce-scatter.9.cloned.1.call-update) | async-done | bytes 81936 | tf_op jit(solution)/shard_map/reduce_scatter | solution.py:84
  602.2 5.7 all-to-all-start.3
  608.3 1.5 select_reduce_fusion
  609.9 4.3 all-to-all-done.3
  614.2 1.7 select_reduce_fusion.2
  616.1 1.5 fusion.32
  617.6 21.7 %all-gather.15 = f32[16,2,8]{2,1,0:T(2,128)S(1)} all-gather(f32[1,2,8]{2,1,0:T(2,128)S(1)} %bitcast.356), channel_id=8, replica_groups=mesh['section'=2,'req'=16,'head'=8] {'req'}, dimensions={0}, use_global_device_ids=true | all-gather | bytes 1088 | tf_op jit(solution)/shard_map/all_gather | solution.py:28
  639.3 21.4 %all-gather.16 = f32[16,2,8]{2,1,0:T(2,128)S(1)} all-gather(f32[1,2,8]{2,1,0:T(2,128)S(1)} %bitcast.364), channel_id=9, replica_groups=mesh['section'=2,'req'=16,'head'=8] {'req'}, dimensions={0}, use_global_device_ids=true | all-gather | bytes 1088 | tf_op jit(solution)/shard_map/all_gather | solution.py:28
  660.8 24.0 %all-gather.8 = f32[32,8,128]{2,1,0:T(8,128)S(1)} all-gather(f32[2,8,128]{2,1,0:T(8,128)S(1)} %fusion.32), channel_id=10, replica_groups=mesh['section'=2,'req'=16,'head'=8] {'req'}, dimensions={0}, use_global_device_ids=true | all-gather | bytes 139264 | tf_op jit(solution)/shard_map/all_gather | solution.py:28
  684.7 1.7 while.102
  687.1 1.6 fusion.26
  688.7 13.1 %all_to_all.50 = bf16[16,16,1024]{2,1,0:T(8,128)(2,1)S(1)} all-to-all(bf16[16,16,1024]{2,1,0:T(8,128)(2,1)S(1)} %tile.54), channel_id=1, replica_groups=mesh['section'=2,'req'=16,'head'=8] {'req'}, dimensions={0} | all-to-all | bytes 1048576 | tf_op jit(solution)/shard_map/all_to_all | solution.py:21
  701.8 1.3 fusion.28
  703.2 73.2 %all-reduce.9.cloned.1.call-done = f32[256,512]{1,0:T(8,128)} async-done(((f32[256,512]{1,0:T(8,128)}), f32[256,512]{1,0:T(8,128)}) %all-reduce.9.cloned.1.call-update) | async-done | bytes 524304 | tf_op jit(solution)/shard_map/psum | solution.py:93
  777.5 23.0 %all-gather.17 = f32[16,1,256]{2,1,0:T(1,128)S(1)} all-gather(f32[1,1,256]{2,1,0:T(1,128)S(1)} %bitcast.367), channel_id=11, replica_groups=mesh['section'=2,'req'=16,'head'=8] {'req'}, dimensions={0}, use_global_device_ids=true | all-gather | bytes 17408 | tf_op jit(solution)/shard_map/all_gather | solution.py:28
  801.3 5.0 fusion.54
  806.4 77.7 %reduce-scatter.11.cloned.1.call-done = f32[16,3584]{1,0:T(8,128)} async-done(((f32[256,3584]{1,0:T(8,128)}), f32[16,3584]{1,0:T(8,128)}) %reduce-scatter.11.cloned.1.call-update) | async-done | bytes 229392 | tf_op jit(solution)/shard_map/reduce_scatter | solution.py:84
  885.2 17.5 %all_to_all.51 = bf16[16,16,1792]{2,1,0:T(8,128)(2,1)S(1)} all-to-all(bf16[16,16,1792]{2,1,0:T(8,128)(2,1)S(1)} %tile.55), channel_id=1, replica_groups=mesh['section'=2,'req'=16,'head'=8] {'req'}, dimensions={0} | all-to-all | bytes 1835008 | tf_op jit(solution)/shard_map/all_to_all | solution.py:21
  902.7 1.4 fusion.12
  904.2 73.2 %all-reduce.11.cloned.1.call-done = f32[256,512]{1,0:T(8,128)} async-done(((f32[256,512]{1,0:T(8,128)}), f32[256,512]{1,0:T(8,128)}) %all-reduce.11.cloned.1.call-update) | async-done | bytes 524304 | tf_op jit(solution)/shard_map/psum | solution.py:93
  977.4 1.9 fusion.53
  (363 shorter events, 25.1 us)
Async XLA Ops:
  6.5 411.9 %copy-start = (bf16[1,1792,512]{2,1,0:T(8,128)(2,1)S(1)}, bf16[1,1792,512]{2,1,0:T(8,128)(2,1)}, u32[]{:S(2)}) copy-start(bf16[1,1792,512]{2,1,0:T(8,128)(2,1)} %param.29) | copy-start | bytes 5505028
  6.5 108.0 %reduce-scatter.5.cloned.1.call-start = ((), (), s32[]{:S(2)}) async-start(), calls=%async_computation.10 | async-start | bytes 1392640 | tf_op jit(solution)/shard_map/reduce_scatter | solution.py:84
  32.5 3.1 copy-start.8
  32.5 3.6 copy-start.9
  117.9 11.9 %all-to-all-start = ((bf16[16,2,512]{2,1,0:T(2,128)(2,1)}), bf16[16,2,512]{2,1,0:T(2,128)(2,1)S(1)}, u32[]{:S(2)}, u32[]{:S(2)}) async-start(bf16[16,2,512]{2,1,0:T(2,128)(2,1)} %reshape.857), calls=%async_computation.1 | async-start | bytes 65536 | tf_op jit(solution)/shard_map/all_to_all | solution.py:21
  123.6 168.3 %all-reduce.5.cloned.1.call-start = ((), (), s32[]{:S(2)}) async-start(), calls=%async_computation.11 | async-start | bytes 1048576 | tf_op jit(solution)/shard_map/psum | solution.py:93
  202.6 14.8 %copy-start.3 = (bf16[1,1,1024,512]{3,2,1,0:T(8,128)(2,1)S(1)}, bf16[1,1,1024,512]{3,2,1,0:T(8,128)(2,1)}, u32[]{:S(2)}) copy-start(bf16[1,1,1024,512]{3,2,1,0:T(8,128)(2,1)} %param.26) | copy-start | bytes 3145732
  218.6 181.2 %reduce-scatter.7.cloned.1.call-start = ((), (), s32[]{:S(2)}) async-start(), calls=%async_computation.12 | async-start | bytes 3899392 | tf_op jit(solution)/shard_map/reduce_scatter | solution.py:84
  218.7 4.5 copy-start.7
  218.7 73.2 %copy-start.2 = (bf16[256,512]{1,0:T(8,128)(2,1)S(1)}, bf16[256,512]{1,0:T(8,128)(2,1)}, u32[]{:S(2)}) copy-start(bf16[256,512]{1,0:T(8,128)(2,1)} %param.23) | copy-start | bytes 786436
  293.1 28.8 %copy-start.5 = (bf16[256,512]{1,0:T(8,128)(2,1)}, bf16[256,512]{1,0:T(8,128)(2,1)S(1)}, u32[]{:S(2)}) copy-start(bf16[256,512]{1,0:T(8,128)(2,1)S(1)} %get-tuple-element.863) | copy-start | bytes 786436
  321.9 171.1 %all-reduce.7.cloned.1.call-start = ((), (), s32[]{:S(2)}) async-start(), calls=%async_computation.13 | async-start | bytes 1048576 | tf_op jit(solution)/shard_map/psum | solution.py:93
  419.8 102.4 %copy-start.1 = (bf16[1,512,1,1280]{3,1,2,0:T(8,128)(2,1)S(1)}, bf16[1,512,1,1280]{3,1,2,0:T(8,128)(2,1)}, u32[]{:S(2)}) copy-start(bf16[1,512,1,1280]{3,1,2,0:T(8,128)(2,1)} %param.25) | copy-start | bytes 3932164
  419.8 179.7 %reduce-scatter.9.cloned.1.call-start = ((), (), s32[]{:S(2)}) async-start(), calls=%async_computation.14 | async-start | bytes 1392640 | tf_op jit(solution)/shard_map/reduce_scatter | solution.py:84
  494.9 2.8 collective-permute-start
  602.2 11.9 %all-to-all-start.3 = ((bf16[16,2,512]{2,1,0:T(2,128)(2,1)}), bf16[16,2,512]{2,1,0:T(2,128)(2,1)S(1)}, u32[]{:S(2)}, u32[]{:S(2)}) async-start(bf16[16,2,512]{2,1,0:T(2,128)(2,1)} %reshape.859), calls=%async_computation.6 | async-start | bytes 65536 | tf_op jit(solution)/shard_map/all_to_all | solution.py:21
  607.9 168.5 %all-reduce.9.cloned.1.call-start = ((), (), s32[]{:S(2)}) async-start(), calls=%async_computation.15 | async-start | bytes 1048576 | tf_op jit(solution)/shard_map/psum | solution.py:93
  687.1 14.8 %copy-start.4 = (bf16[1,1,1024,512]{3,2,1,0:T(8,128)(2,1)S(1)}, bf16[1,1,1024,512]{3,2,1,0:T(8,128)(2,1)}, u32[]{:S(2)}) copy-start(bf16[1,1,1024,512]{3,2,1,0:T(8,128)(2,1)} %param.26) | copy-start | bytes 3145732
  688.7 87.7 %copy-start.6 = (bf16[256,512]{1,0:T(8,128)(2,1)S(1)}, bf16[256,512]{1,0:T(8,128)(2,1)}, u32[]{:S(2)}) copy-start(bf16[256,512]{1,0:T(8,128)(2,1)} %get-tuple-element.861) | copy-start | bytes 786436
  703.1 181.0 %reduce-scatter.11.cloned.1.call-start = ((), (), s32[]{:S(2)}) async-start(), calls=%async_computation.16 | async-start | bytes 3899392 | tf_op jit(solution)/shard_map/reduce_scatter | solution.py:84
  806.3 171.0 %all-reduce.11.cloned.1.call-start = ((), (), s32[]{:S(2)}) async-start(), calls=%async_computation.17 | async-start | bytes 1048576 | tf_op jit(solution)/shard_map/psum | solution.py:93
Sparse Core Ops, SparseCore 0:
  35.7 78.7 reduce-scatter.4
  218.7 73.0 all-reduce.4
  322.0 77.7 reduce-scatter.6
  420.0 73.0 all-reduce.6
  524.9 74.5 reduce-scatter.8
  703.2 73.0 all-reduce.8
  806.5 77.6 reduce-scatter.10
  904.3 73.0 all-reduce.10
